TPU v7x, 128 devices: a whole 4x4x4 slice. The times are simulated.
128 devices in a mesh: wide: 16 (over x, z), narrow: 8 (over y, core).
Axes of the slice: x: 4, y: 4, z: 4, core: 2. Of those that a mesh axis runs over, the one named last changes fastest.
Arguments:
- aperture: float32 [256, 128, 128], P(('wide', 'narrow')), may hold values from 0.8 to 2.5
- pressure: float32 [256, 128, 128], P(('wide', 'narrow')), may hold values from -6 to 6
- adj_source: float32 [256, 128, 128], P(('wide', 'narrow')), may hold values from -6 to 6
- trace_weight: float32 [8192, 64], P(('wide', 'narrow')), may hold values from 0.2 to 2
- end_device: int32 [8192, 2], P(('wide', 'narrow')), may hold values from 0 to 127, as said below
- end_local: int32 [8192, 2], P(('wide', 'narrow')), may hold values from 0 to 1
- trace_nodes: int32 [8192, 2, 64], P(('wide', 'narrow')), may hold values from 0 to 16383
Outputs:
- aperture_grad: float32 [256, 128, 128], P(('wide', 'narrow'))
- adjoint: float32 [256, 128, 128], P(('wide', 'narrow'))
Inputs may be any that keep to these rules, and one draw needn't show every extreme that they name: `end_device`: the two ends of an intersection lie on different devices. Of the ends of the intersections owned by one device, every device holds none or exactly 2. Any two devices are joined by at most 2 intersections over all owners, and some pairs by exactly 2. `trace_nodes`: several trace nodes may share a cell.
All inputs are finite; a program needn't handle non-finite values.
Results may differ from a plain program's by a relative error of at most 0.0022.
Values sent between devices are 32-bit elements; how exact they have to be, the bound alone decides.
A program may use at most 64 MiB of HBM per device.

v0:
```python
import jax
import jax.numpy as jnp
from jax import lax
from jax.sharding import PartitionSpec as P

SWEEPS = 3
INNER = 8


LEAKAGE = 0.25
HIGH = lax.Precision.HIGHEST


def neighbours(field, face_x, face_y):
    total = jnp.pad(face_x * field[:, 1:, :], ((0, 0), (0, 1), (0, 0)))
    total = total + jnp.pad(face_x * field[:, :-1, :], ((0, 0), (1, 0), (0, 0)))
    total = total + jnp.pad(face_y * field[:, :, 1:], ((0, 0), (0, 0), (0, 1)))
    total = total + jnp.pad(face_y * field[:, :, :-1], ((0, 0), (0, 0), (1, 0)))
    return total


def face_total(face_x, face_y):
    total = jnp.pad(face_x, ((0, 0), (0, 1), (0, 0))) + jnp.pad(face_x, ((0, 0), (1, 0), (0, 0)))
    return (
        total
        + jnp.pad(face_y, ((0, 0), (0, 0), (0, 1)))
        + jnp.pad(face_y, ((0, 0), (0, 0), (1, 0)))
    )


def gradient_of(aperture, pressure, adjoint):
    along_x = (pressure[:, 1:, :] - pressure[:, :-1, :]) * (adjoint[:, 1:, :] - adjoint[:, :-1, :])
    along_y = (pressure[:, :, 1:] - pressure[:, :, :-1]) * (adjoint[:, :, 1:] - adjoint[:, :, :-1])
    return -(aperture * aperture / 8.0) * face_total(along_x, along_y)


def rank_within(target, device_count):
    member = (target[:, None] == jnp.arange(device_count, dtype=jnp.int32)[None, :]).astype(
        jnp.int32
    )
    before = jnp.cumsum(member, axis=0) - member
    return jnp.sum(before * member, axis=1)


def split_pair(values):
    high_part = values.astype(jnp.bfloat16)
    low_part = (values - high_part.astype(jnp.float32)).astype(jnp.bfloat16)
    return (high_part, low_part)


def group_size(device_count, width):
    group = 1
    while device_count % (group * 2) == 0 and group * 2 * width <= 2048:
        group = group * 2
    return group


def scatter_cells(row_index, col_index, values, row_count, grid_size, blocks):
    row_blocks = row_index.reshape(blocks, -1)
    col_blocks = col_index.reshape(blocks, -1)
    value_blocks = values.reshape(blocks, -1)
    row_ids = jnp.arange(row_count, dtype=jnp.int32)
    col_ids = jnp.arange(grid_size, dtype=jnp.int32)
    zero_half = jnp.zeros((), jnp.bfloat16)

    def add_block(total, pieces):
        rows_now, cols_now, vals_now = pieces
        row_hot = (rows_now[None, :] == row_ids[:, None]).astype(jnp.bfloat16)
        col_hot = cols_now[:, None] == col_ids[None, :]
        high_part, low_part = split_pair(vals_now)
        right = jnp.concatenate(
            [
                jnp.where(col_hot, high_part[:, None], zero_half),
                jnp.where(col_hot, low_part[:, None], zero_half),
            ],
            axis=1,
        )
        product = jnp.dot(row_hot, right, preferred_element_type=jnp.float32)
        return (total + product[:, :grid_size] + product[:, grid_size:], None)

    start = jnp.zeros((row_count, grid_size), jnp.float32)
    total, _ = lax.scan(add_block, start, (row_blocks, col_blocks, value_blocks))
    return total


def gather_cells(field_rows, row_index, col_index, blocks):
    row_count, grid_size = field_rows.shape
    high_part, low_part = split_pair(field_rows)
    both_parts = jnp.concatenate([high_part, low_part], axis=1)
    row_ids = jnp.arange(row_count, dtype=jnp.int32)
    col_ids = jnp.arange(grid_size, dtype=jnp.int32)

    def pick_block(carry, pieces):
        rows_now, cols_now = pieces
        row_hot = (rows_now[:, None] == row_ids[None, :]).astype(jnp.bfloat16)
        picked = jnp.dot(row_hot, both_parts, preferred_element_type=jnp.float32)
        merged = picked[:, :grid_size] + picked[:, grid_size:]
        col_hot = cols_now[:, None] == col_ids[None, :]
        return (carry, jnp.sum(jnp.where(col_hot, merged, 0.0), axis=1))

    _, picked_all = lax.scan(
        pick_block, 0, (row_index.reshape(blocks, -1), col_index.reshape(blocks, -1))
    )
    return picked_all.reshape(-1)


def body(aperture, pressure, adj_source, trace_weight, end_device, end_local, trace_nodes):
    frac_count, grid_size, _ = aperture.shape
    owned_count, trace_len = trace_weight.shape
    device_count = lax.axis_size(("wide", "narrow"))
    capacity = owned_count // (device_count // 4)
    end_count = 2 * owned_count
    slot_total = device_count * capacity
    row_width = capacity * trace_len
    blocks = device_count // group_size(device_count, row_width)
    row_count = frac_count * grid_size
    conduct = aperture * aperture * aperture / 12.0
    face_x = (conduct[:, :-1, :] + conduct[:, 1:, :]) * 0.5
    face_y = (conduct[:, :, :-1] + conduct[:, :, 1:]) * 0.5
    destination = end_device.reshape(end_count)
    slot_place = destination * capacity + rank_within(destination, device_count)
    placing = (slot_place[:, None] == jnp.arange(slot_total, dtype=jnp.int32)[None, :]).astype(
        jnp.float32
    )
    cells_own = end_local.reshape(end_count, 1) * (grid_size * grid_size) + trace_nodes.reshape(
        end_count, trace_len
    )
    outgoing = jnp.full((slot_total, trace_len), -1, jnp.int32).at[slot_place].set(cells_own)
    outgoing = outgoing.reshape(device_count, row_width)
    weight_end = jnp.broadcast_to(trace_weight[:, None, :], (owned_count, 2, trace_len)).reshape(
        end_count, trace_len
    )
    weight_out = jnp.einsum("es,et->st", placing, weight_end, precision=HIGH)
    weight_out = weight_out.reshape(device_count, row_width)
    incoming = lax.all_to_all(outgoing, ("wide", "narrow"), split_axis=0, concat_axis=0, tiled=True)
    weight_in = lax.all_to_all(
        weight_out, ("wide", "narrow"), split_axis=0, concat_axis=0, tiled=True
    )
    active_slot = (incoming >= 0).reshape(-1)
    flat_cells = incoming.reshape(-1)
    row_index = jnp.where(active_slot, flat_cells // grid_size, -1)
    col_index = jnp.where(active_slot, flat_cells % grid_size, -1)
    trace_sum = scatter_cells(
        row_index,
        col_index,
        jnp.where(active_slot, weight_in.reshape(-1), 0.0),
        row_count,
        grid_size,
        blocks,
    ).reshape(frac_count, grid_size, grid_size)
    inv_diag = 1.0 / (LEAKAGE + face_total(face_x, face_y) + trace_sum)
    adjoint = adj_source * inv_diag
    for sweep_step in range(SWEEPS):
        values = gather_cells(adjoint.reshape(row_count, grid_size), row_index, col_index, blocks)
        values = values.reshape(device_count, row_width)
        returned = lax.all_to_all(
            values, ("wide", "narrow"), split_axis=0, concat_axis=0, tiled=True
        )
        end_values = jnp.dot(placing, returned.reshape(slot_total, trace_len), precision=HIGH)
        end_values = end_values.reshape(owned_count, 2, trace_len)
        source_end = (trace_weight[:, None, :] * end_values[:, ::-1, :]).reshape(
            end_count, trace_len
        )
        packed = jnp.einsum("es,et->st", placing, source_end, precision=HIGH)
        packed = packed.reshape(device_count, row_width)
        arrived = lax.all_to_all(
            packed, ("wide", "narrow"), split_axis=0, concat_axis=0, tiled=True
        )
        coupling = scatter_cells(
            row_index,
            col_index,
            jnp.where(active_slot, arrived.reshape(-1), 0.0),
            row_count,
            grid_size,
            blocks,
        ).reshape(frac_count, grid_size, grid_size)
        forcing = adj_source + coupling
        for inner_step in range(INNER):
            adjoint = (forcing + neighbours(adjoint, face_x, face_y)) * inv_diag
    return (gradient_of(aperture, pressure, adjoint), adjoint)


def solution(mesh):
    placed = (
        P(("wide", "narrow"), None, None),
        P(("wide", "narrow"), None, None),
        P(("wide", "narrow"), None, None),
        P(("wide", "narrow"), None),
        P(("wide", "narrow"), None),
        P(("wide", "narrow"), None),
        P(("wide", "narrow"), None, None),
    )
    return jax.shard_map(
        body,
        mesh=mesh,
        in_specs=placed,
        out_specs=(P(("wide", "narrow"), None, None), P(("wide", "narrow"), None, None)),
        check_vma=False,
    )
```

profile of v0, /device:TPU:1, one launch (start us, length us, event | category | flops | bytes accessed | tf_op | source)
XLA Modules:
  0.0 251.6 jit_solution(13512445396820417994)
XLA Ops:
  3.9 11.5 %all-to-all-start.1 = ((f32[128,1,128]{2,1,0:T(1,128)}), f32[128,1,128]{2,1,0:T(1,128)S(1)}, u32[]{:S(2)}, u32[]{:S(2)}) async-start(f32[128,1,128]{2,1,0:T(1,128)} %bitcast.6), calls=%async_computation.1 | async-start | bytes 131072 | tf_op jit(solution)/shard_map/all_to_all | solution.py:136
  19.6 5.1 %all-to-all-done.1 = f32[128,1,128]{2,1,0:T(1,128)S(1)} async-done(((f32[128,1,128]{2,1,0:T(1,128)}), f32[128,1,128]{2,1,0:T(1,128)S(1)}, u32[]{:S(2)}, u32[]{:S(2)}) %all-to-all-start.1) | async-done | bytes 65568 | tf_op jit(solution)/shard_map/all_to_all | solution.py:136
  24.8 4.6 %all-to-all-start = ((s32[128,1,128]{2,1,0:T(1,128)}), s32[128,1,128]{2,1,0:T(1,128)S(1)}, u32[]{:S(2)}, u32[]{:S(2)}) async-start(s32[128,1,128]{2,1,0:T(1,128)} %bitcast.3), calls=%async_computation | async-start | bytes 131072 | tf_op jit(solution)/shard_map/all_to_all | solution.py:135
  30.8 8.0 %all-to-all-done = s32[128,1,128]{2,1,0:T(1,128)S(1)} async-done(((s32[128,1,128]{2,1,0:T(1,128)}), s32[128,1,128]{2,1,0:T(1,128)S(1)}, u32[]{:S(2)}, u32[]{:S(2)}) %all-to-all-start) | async-done | bytes 65568 | tf_op jit(solution)/shard_map/all_to_all | solution.py:135
  40.3 17.9 %while.80 = (s32[]{:T(128)}, f32[256,128]{1,0:T(8,128)S(1)}, s32[8,2048]{1,0:T(8,128)S(1)}, s32[8,2048]{1,0:T(8,128)S(1)}, f32[8,2048]{1,0:T(8,128)S(1)}, /*index=5*/s32[]{:T(128)}, s32[]{:T(128)}) while((s32[]{:T(128)}, f32[256,128]{1,0:T(8,128)S(1)}, s32[8,2048]{1,0:T(8,128)S(1)}, s32[8,2048]{1,0:T(8,128)S(1)}, ...), condition=%wide.region_4.5_spmd.clone, body=%wide.region_3.4_spmd.clone.sunk | while | flops 271949824 | bytes 2973791 | solution.py:82
  40.4 1.6 fusion.153
  42.6 1.6 fusion.153
  44.8 1.6 fusion.153
  47.1 1.6 fusion.153
  49.3 1.6 fusion.153
  51.6 1.6 fusion.153
  53.8 1.6 fusion.153
  56.0 1.6 fusion.153
  58.4 12.0 %while.77 = (s32[]{:T(128)}, f32[8,2048]{1,0:T(8,128)S(1)}, s32[8,2048]{1,0:T(8,128)S(1)}, s32[8,2048]{1,0:T(8,128)S(1)}, bf16[256,256]{1,0:T(8,128)(2,1)S(1)}, /*index=5*/s32[]{:T(128)}, s32[]{:T(128)}) while((s32[]{:T(128)}, f32[8,2048]{1,0:T(8,128)S(1)}, s32[8,2048]{1,0:T(8,128)S(1)}, s32[8,2048]{1,0:T(8,128)S(1)}, ...), condition=%wide.region_7.8_spmd.clone, body=%wide.region_5.7_spmd.clone.sunk | while | flops 270006272 | bytes 4399189 | solution.py:101
  71.1 4.6 %all-to-all-start.2 = ((f32[128,1,128]{2,1,0:T(1,128)}), f32[128,1,128]{2,1,0:T(1,128)S(1)}, u32[]{:S(2)}, u32[]{:S(2)}) async-start(f32[128,1,128]{2,1,0:T(1,128)} %all_to_all.55), calls=%async_computation.2 | async-start | bytes 131072 | tf_op jit(solution)/shard_map/all_to_all | solution.py:156
  75.8 9.4 %all-to-all-done.2 = f32[128,1,128]{2,1,0:T(1,128)S(1)} async-done(((f32[128,1,128]{2,1,0:T(1,128)}), f32[128,1,128]{2,1,0:T(1,128)S(1)}, u32[]{:S(2)}, u32[]{:S(2)}) %all-to-all-start.2) | async-done | bytes 65568 | tf_op jit(solution)/shard_map/all_to_all | solution.py:156
  87.4 4.6 %all-to-all-start.3 = ((f32[128,1,128]{2,1,0:T(1,128)}), f32[128,1,128]{2,1,0:T(1,128)S(1)}, u32[]{:S(2)}, u32[]{:S(2)}) async-start(f32[128,1,128]{2,1,0:T(1,128)} %bitcast.11), calls=%async_computation.3 | async-start | bytes 131072 | tf_op jit(solution)/shard_map/all_to_all | solution.py:166
  92.2 9.3 %all-to-all-done.3 = f32[128,1,128]{2,1,0:T(1,128)S(1)} async-done(((f32[128,1,128]{2,1,0:T(1,128)}), f32[128,1,128]{2,1,0:T(1,128)S(1)}, u32[]{:S(2)}, u32[]{:S(2)}) %all-to-all-start.3) | async-done | bytes 65568 | tf_op jit(solution)/shard_map/all_to_all | solution.py:166
  102.2 17.9 %while.81 = (s32[]{:T(128)}, f32[256,128]{1,0:T(8,128)S(1)}, s32[8,2048]{1,0:T(8,128)S(1)}, s32[8,2048]{1,0:T(8,128)S(1)}, f32[8,2048]{1,0:T(8,128)S(1)}, /*index=5*/s32[]{:T(128)}, s32[]{:T(128)}) while((s32[]{:T(128)}, f32[256,128]{1,0:T(8,128)S(1)}, s32[8,2048]{1,0:T(8,128)S(1)}, s32[8,2048]{1,0:T(8,128)S(1)}, ...), condition=%wide.region_9.10_spmd.clone, body=%wide.region_8.9_spmd.clone.sunk | while | flops 271949824 | bytes 2973791 | solution.py:82
  102.3 1.6 fusion.156
  104.5 1.6 fusion.156
  106.8 1.6 fusion.156
  109.0 1.6 fusion.156
  111.2 1.6 fusion.156
  113.5 1.6 fusion.156
  115.7 1.6 fusion.156
  118.0 1.6 fusion.156
  122.4 12.0 %while.78 = (s32[]{:T(128)}, f32[8,2048]{1,0:T(8,128)S(1)}, s32[8,2048]{1,0:T(8,128)S(1)}, s32[8,2048]{1,0:T(8,128)S(1)}, bf16[256,256]{1,0:T(8,128)(2,1)S(1)}, /*index=5*/s32[]{:T(128)}, s32[]{:T(128)}) while((s32[]{:T(128)}, f32[8,2048]{1,0:T(8,128)S(1)}, s32[8,2048]{1,0:T(8,128)S(1)}, s32[8,2048]{1,0:T(8,128)S(1)}, ...), condition=%wide.region_12.13_spmd.clone, body=%wide.region_10.12_spmd.clone.sunk | while | flops 270006272 | bytes 4399189 | solution.py:101
  135.1 4.6 %all-to-all-start.4 = ((f32[128,1,128]{2,1,0:T(1,128)}), f32[128,1,128]{2,1,0:T(1,128)S(1)}, u32[]{:S(2)}, u32[]{:S(2)}) async-start(f32[128,1,128]{2,1,0:T(1,128)} %all_to_all.59), calls=%async_computation.4 | async-start | bytes 131072 | tf_op jit(solution)/shard_map/all_to_all | solution.py:156
  139.8 9.4 %all-to-all-done.4 = f32[128,1,128]{2,1,0:T(1,128)S(1)} async-done(((f32[128,1,128]{2,1,0:T(1,128)}), f32[128,1,128]{2,1,0:T(1,128)S(1)}, u32[]{:S(2)}, u32[]{:S(2)}) %all-to-all-start.4) | async-done | bytes 65568 | tf_op jit(solution)/shard_map/all_to_all | solution.py:156
  151.4 4.6 %all-to-all-start.5 = ((f32[128,1,128]{2,1,0:T(1,128)}), f32[128,1,128]{2,1,0:T(1,128)S(1)}, u32[]{:S(2)}, u32[]{:S(2)}) async-start(f32[128,1,128]{2,1,0:T(1,128)} %bitcast.16), calls=%async_computation.5 | async-start | bytes 131072 | tf_op jit(solution)/shard_map/all_to_all | solution.py:166
  156.2 9.3 %all-to-all-done.5 = f32[128,1,128]{2,1,0:T(1,128)S(1)} async-done(((f32[128,1,128]{2,1,0:T(1,128)}), f32[128,1,128]{2,1,0:T(1,128)S(1)}, u32[]{:S(2)}, u32[]{:S(2)}) %all-to-all-start.5) | async-done | bytes 65568 | tf_op jit(solution)/shard_map/all_to_all | solution.py:166
  166.2 17.9 %while.82 = (s32[]{:T(128)}, f32[256,128]{1,0:T(8,128)S(1)}, s32[8,2048]{1,0:T(8,128)S(1)}, s32[8,2048]{1,0:T(8,128)S(1)}, f32[8,2048]{1,0:T(8,128)S(1)}, /*index=5*/s32[]{:T(128)}, s32[]{:T(128)}) while((s32[]{:T(128)}, f32[256,128]{1,0:T(8,128)S(1)}, s32[8,2048]{1,0:T(8,128)S(1)}, s32[8,2048]{1,0:T(8,128)S(1)}, ...), condition=%wide.region_14.15_spmd.clone, body=%wide.region_13.14_spmd.clone.sunk | while | flops 271949824 | bytes 2973791 | solution.py:82
  166.3 1.6 fusion.159
  168.5 1.6 fusion.159
  170.8 1.6 fusion.159
  173.0 1.6 fusion.159
  175.2 1.6 fusion.159
  177.5 1.6 fusion.159
  179.7 1.6 fusion.159
  182.0 1.6 fusion.159
  186.4 12.0 %while.79 = (s32[]{:T(128)}, f32[8,2048]{1,0:T(8,128)S(1)}, s32[8,2048]{1,0:T(8,128)S(1)}, s32[8,2048]{1,0:T(8,128)S(1)}, bf16[256,256]{1,0:T(8,128)(2,1)S(1)}, /*index=5*/s32[]{:T(128)}, s32[]{:T(128)}) while((s32[]{:T(128)}, f32[8,2048]{1,0:T(8,128)S(1)}, s32[8,2048]{1,0:T(8,128)S(1)}, s32[8,2048]{1,0:T(8,128)S(1)}, ...), condition=%wide.region_17.18_spmd.clone, body=%wide.region_15.17_spmd.clone.sunk | while | flops 270006272 | bytes 4399189 | solution.py:101
  199.1 4.5 %all-to-all-start.6 = ((f32[128,1,128]{2,1,0:T(1,128)}), f32[128,1,128]{2,1,0:T(1,128)S(1)}, u32[]{:S(2)}, u32[]{:S(2)}) async-start(f32[128,1,128]{2,1,0:T(1,128)} %all_to_all.63), calls=%async_computation.6 | async-start | bytes 131072 | tf_op jit(solution)/shard_map/all_to_all | solution.py:156
  203.7 9.4 %all-to-all-done.6 = f32[128,1,128]{2,1,0:T(1,128)S(1)} async-done(((f32[128,1,128]{2,1,0:T(1,128)}), f32[128,1,128]{2,1,0:T(1,128)S(1)}, u32[]{:S(2)}, u32[]{:S(2)}) %all-to-all-start.6) | async-done | bytes 65568 | tf_op jit(solution)/shard_map/all_to_all | solution.py:156
  215.3 4.6 %all-to-all-start.7 = ((f32[128,1,128]{2,1,0:T(1,128)}), f32[128,1,128]{2,1,0:T(1,128)S(1)}, u32[]{:S(2)}, u32[]{:S(2)}) async-start(f32[128,1,128]{2,1,0:T(1,128)} %bitcast.21), calls=%async_computation.7 | async-start | bytes 131072 | tf_op jit(solution)/shard_map/all_to_all | solution.py:166
  220.1 9.3 %all-to-all-done.7 = f32[128,1,128]{2,1,0:T(1,128)S(1)} async-done(((f32[128,1,128]{2,1,0:T(1,128)}), f32[128,1,128]{2,1,0:T(1,128)S(1)}, u32[]{:S(2)}, u32[]{:S(2)}) %all-to-all-start.7) | async-done | bytes 65568 | tf_op jit(solution)/shard_map/all_to_all | solution.py:166
  230.1 17.9 %while.83 = (s32[]{:T(128)}, f32[256,128]{1,0:T(8,128)S(1)}, s32[8,2048]{1,0:T(8,128)S(1)}, s32[8,2048]{1,0:T(8,128)S(1)}, f32[8,2048]{1,0:T(8,128)S(1)}, /*index=5*/s32[]{:T(128)}, s32[]{:T(128)}) while((s32[]{:T(128)}, f32[256,128]{1,0:T(8,128)S(1)}, s32[8,2048]{1,0:T(8,128)S(1)}, s32[8,2048]{1,0:T(8,128)S(1)}, ...), condition=%wide.region_19.20_spmd.clone, body=%wide.region_18.19_spmd.clone.sunk | while | flops 271949824 | bytes 2973791 | solution.py:82
  230.2 1.6 fusion.162
  (425 shorter events, 93.8 us)
Async XLA Ops:
  3.9 20.9 %all-to-all-start.1 = ((f32[128,1,128]{2,1,0:T(1,128)}), f32[128,1,128]{2,1,0:T(1,128)S(1)}, u32[]{:S(2)}, u32[]{:S(2)}) async-start(f32[128,1,128]{2,1,0:T(1,128)} %bitcast.6), calls=%async_computation.1 | async-start | bytes 131072 | tf_op jit(solution)/shard_map/all_to_all | solution.py:136
  24.8 14.0 %all-to-all-start = ((s32[128,1,128]{2,1,0:T(1,128)}), s32[128,1,128]{2,1,0:T(1,128)S(1)}, u32[]{:S(2)}, u32[]{:S(2)}) async-start(s32[128,1,128]{2,1,0:T(1,128)} %bitcast.3), calls=%async_computation | async-start | bytes 131072 | tf_op jit(solution)/shard_map/all_to_all | solution.py:135
  40.3 17.9 %copy-start.1 = (f32[2,128,128]{2,1,0:T(8,128)S(1)}, f32[2,128,128]{2,1,0:T(8,128)}, u32[]{:S(2)}) copy-start(f32[2,128,128]{2,1,0:T(8,128)} %param.23) | copy-start | bytes 393220
  58.4 27.8 %copy-start.3 = (f32[64,64]{1,0:T(8,128)S(1)}, f32[64,64]{1,0:T(8,128)}, u32[]{:S(2)}) copy-start(f32[64,64]{1,0:T(8,128)} %param.24) | copy-start | bytes 49156
  71.1 14.0 %all-to-all-start.2 = ((f32[128,1,128]{2,1,0:T(1,128)}), f32[128,1,128]{2,1,0:T(1,128)S(1)}, u32[]{:S(2)}, u32[]{:S(2)}) async-start(f32[128,1,128]{2,1,0:T(1,128)} %all_to_all.55), calls=%async_computation.2 | async-start | bytes 131072 | tf_op jit(solution)/shard_map/all_to_all | solution.py:156
  87.4 14.0 %all-to-all-start.3 = ((f32[128,1,128]{2,1,0:T(1,128)}), f32[128,1,128]{2,1,0:T(1,128)S(1)}, u32[]{:S(2)}, u32[]{:S(2)}) async-start(f32[128,1,128]{2,1,0:T(1,128)} %bitcast.11), calls=%async_computation.3 | async-start | bytes 131072 | tf_op jit(solution)/shard_map/all_to_all | solution.py:166
  135.1 14.1 %all-to-all-start.4 = ((f32[128,1,128]{2,1,0:T(1,128)}), f32[128,1,128]{2,1,0:T(1,128)S(1)}, u32[]{:S(2)}, u32[]{:S(2)}) async-start(f32[128,1,128]{2,1,0:T(1,128)} %all_to_all.59), calls=%async_computation.4 | async-start | bytes 131072 | tf_op jit(solution)/shard_map/all_to_all | solution.py:156
  151.4 14.0 %all-to-all-start.5 = ((f32[128,1,128]{2,1,0:T(1,128)}), f32[128,1,128]{2,1,0:T(1,128)S(1)}, u32[]{:S(2)}, u32[]{:S(2)}) async-start(f32[128,1,128]{2,1,0:T(1,128)} %bitcast.16), calls=%async_computation.5 | async-start | bytes 131072 | tf_op jit(solution)/shard_map/all_to_all | solution.py:166
  199.1 14.0 %all-to-all-start.6 = ((f32[128,1,128]{2,1,0:T(1,128)}), f32[128,1,128]{2,1,0:T(1,128)S(1)}, u32[]{:S(2)}, u32[]{:S(2)}) async-start(f32[128,1,128]{2,1,0:T(1,128)} %all_to_all.63), calls=%async_computation.6 | async-start | bytes 131072 | tf_op jit(solution)/shard_map/all_to_all | solution.py:156
  215.3 14.0 %all-to-all-start.7 = ((f32[128,1,128]{2,1,0:T(1,128)}), f32[128,1,128]{2,1,0:T(1,128)S(1)}, u32[]{:S(2)}, u32[]{:S(2)}) async-start(f32[128,1,128]{2,1,0:T(1,128)} %bitcast.21), calls=%async_computation.7 | async-start | bytes 131072 | tf_op jit(solution)/shard_map/all_to_all | solution.py:166
  249.7 0.9 copy-start.2
  250.0 0.9 copy-start.4
  250.6 1.0 copy-start
where the time goes:
time: 252 us
  other arithmetic  76.6 us (30%)
  waiting for transfers between devices  69.1 us (27%)
  starting transfers between devices  43.7 us (17%)
  matrix products  41.5 us (16%)
  local copies, waits for them, and re-layouts  16.2 us (6%)
  loops' own time  2.86 us (1%)
    select_n x32, other arithmetic, add_block(): jnp.where(col_hot, high_part[:, None], zero_half)  51.9 us
    all_to_all x3, waiting for transfers between devices, body(): lax.all_to_all(values, ('wide', 'narrow'), split_axis=0, concat_axis=0, t...  28.1 us
    all_to_all x3, waiting for transfers between devices, body(): lax.all_to_all(packed, ('wide', 'narrow'), split_axis=0, concat_axis=0, t...  27.8 us
    dot_general x24, matrix products, pick_block(): picked = jnp.dot(row_hot, both_parts, preferred_element_type=jnp.float32)  25 us
    dot_general x32, matrix products, add_block(): product = jnp.dot(row_hot, right, preferred_element_type=jnp.float32)  14.3 us
    all_to_all x3, starting transfers between devices, body(): lax.all_to_all(packed, ('wide', 'narrow'), split_axis=0, concat_axis=0, t...  13.8 us
    all_to_all x3, starting transfers between devices, body(): lax.all_to_all(values, ('wide', 'narrow'), split_axis=0, concat_axis=0, t...  13.8 us
    all_to_all x1, starting transfers between devices, body(): lax.all_to_all(weight_out, ('wide', 'narrow'), split_axis=0, concat_axis=...  11.5 us
  transfers between devices with their start and end apart: 8, of which 8 were waited for; matrix products, arithmetic and copies ran while one was open for 2% of the time, Pallas kernels for 0%

commit v1 on v0

v1 whole, which is shorter than its diff:
```python
import itertools

import jax
import jax.numpy as jnp
import numpy as np
from jax import lax
from jax.experimental import pallas as pl
from jax.experimental.pallas import tpu as pltpu
from jax.sharding import PartitionSpec as P

SWEEPS = 3
INNER = 8
LEAKAGE = 0.25
F32 = jnp.float32
BF16 = jnp.bfloat16
MESH = pl.DeviceIdType.MESH
DEV = 128
ROWS = 8
CHUNKS = DEV // ROWS


def negated(offset):
    return tuple(-d % 4 for d in offset[:3]) + (offset[3],)


def hops(offset):
    return sum(min(d, 4 - d) for d in offset[:3])


def far_first():
    order = []
    for offset in sorted(itertools.product(range(4), range(4), range(4), range(2)), key=lambda o: (-hops(o), o)):
        if offset not in order and negated(offset) != offset:
            order += [offset, negated(offset)]
    for offset in itertools.product((0, 2), (0, 2), (0, 2), (0, 1)):
        order.append(offset)
    order.sort(key=lambda o: (-hops(o), o == (0, 0, 0, 0)))
    return order


ORDER = far_first()
BACK = [ORDER.index(negated(o)) for o in ORDER]
assert all(b // ROWS == i // ROWS for i, b in enumerate(BACK))


def codes():
    return np.array([((o[0] * 4 + o[1]) * 4 + o[2]) * 2 + o[3] for o in ORDER], np.int32)


def device_at(offset, wide, narrow):
    dx, dz, dy, dc = offset
    return (
        ((wide // 4 + dx) % 4) * 4 + (wide % 4 + dz) % 4,
        ((narrow // 2 + dy) % 4) * 2 + (narrow % 2 + dc) % 2,
    )


def moved(code, me):
    x = ((code >> 5) + (me // 32)) & 3
    z = ((code >> 3) + (me // 8)) & 3
    y = ((code >> 1) + (me // 2)) & 3
    c = (code + me) & 1
    return x * 32 + z * 8 + y * 2 + c


def iota(shape, axis):
    return lax.broadcasted_iota(jnp.int32, shape, axis)


def wait_bytes(ref, sem):
    pltpu.make_async_copy(ref, ref, sem).wait()


def dot(a, b, ca=1, cb=0):
    return lax.dot_general(a, b, (((ca,), (cb,)), ((), ())), preferred_element_type=F32)


def hilo(x):
    high = x.astype(BF16)
    return high, (x - high.astype(F32)).astype(BF16)


def kernel(
    ap_h, pr_h, src_h, tw_h, ed_h, el_h, tn_h, kc_h, kr_h,
    grad_h, adj_h,
    ap, pr, src, tw, ed, el, tn, kc, kr, in_sem, out_sem,
    msg, rmsg, snd, rcv, m_send, m_recv, v_send, v_recv,
    hot, row1, col, wgt, adj, cup, cdn, clf, crt, inv, acc, grad,
):
    wide = lax.axis_index("wide")
    narrow = lax.axis_index("narrow")
    me = wide * 8 + narrow
    barrier = pltpu.get_barrier_semaphore()
    for offset in ORDER[:-1]:
        pl.semaphore_signal(barrier, inc=1, device_id=device_at(offset, wide, narrow), device_id_type=MESH)
    pairs = [(ed_h, ed), (el_h, el), (tn_h, tn), (tw_h, tw), (kc_h, kc), (kr_h, kr), (ap_h, ap), (src_h, src), (pr_h, pr)]
    loads = [pltpu.make_async_copy(a, b, in_sem.at[i]) for i, (a, b) in enumerate(pairs)]
    for load in loads:
        load.start()
    for load in loads[:6]:
        load.wait()

    at_col = moved(kc[...], me)
    at_row = moved(kr[...], me)[0:1, :].astype(F32)
    lane = iota((DEV, 128), 1)
    member = [jnp.where(at_col[:, :64] == ed[e : e + 1, :], 1.0, 0.0) for e in range(2)]
    earlier = jnp.where(iota((64, 64), 0) < iota((64, 64), 1), 1.0, 0.0).astype(BF16)
    before = dot((member[0] + member[1]).astype(BF16), earlier)
    place = [[jnp.where(before == float(s), member[e], 0.0) for e in range(2)] for s in range(2)]
    left = jnp.concatenate([place[s][e] for s in range(2) for e in range(2)], axis=1).astype(BF16)
    weight_parts = hilo(tw[...])
    right = []
    zero = jnp.zeros((64, 64), BF16)
    for s in range(2):
        for e in range(2):
            nodes = tn[:, e, :]
            parts = [((nodes >> 7) + 1).astype(F32).astype(BF16), (nodes & 127).astype(F32).astype(BF16), *weight_parts]
            right.append(
                jnp.concatenate([jnp.concatenate([x, zero] if s == 0 else [zero, x], axis=1) for x in parts], axis=1)
            )
    out = dot(left, jnp.concatenate(right, axis=0))

    def picked(s, rows):
        return sum(jnp.sum(place[s][e] * rows[e], axis=1, keepdims=True) for e in range(2))

    local_rows = [el[e : e + 1, :].astype(F32) for e in range(2)]
    other_rows = [ed[1 - e : 2 - e, :].astype(F32) + 1.0 for e in range(2)]
    local = jnp.where(lane < 64, picked(0, local_rows), picked(1, local_rows))
    cells = (out[:, 0:128] - 1.0 + 128.0 * local) * 128.0 + out[:, 128:256] + 1.0
    msg[:, 0, 0:128] = jnp.where(out[:, 0:128] > 0.5, cells, 0.0)
    msg[:, 0, 128:256] = out[:, 256:384] + out[:, 384:512]
    msg[:, 0, 256:384] = jnp.where(lane == 0, picked(0, other_rows), jnp.where(lane == 1, picked(1, other_rows), 0.0))

    pl.semaphore_wait(barrier, DEV - 1)
    for i, offset in enumerate(ORDER[:-1]):
        pltpu.make_async_remote_copy(
            src_ref=msg.at[i],
            dst_ref=rmsg.at[BACK[i]],
            send_sem=m_send,
            recv_sem=m_recv,
            device_id=device_at(offset, wide, narrow),
            device_id_type=MESH,
        ).start()
    rmsg[DEV - 1] = msg[DEV - 1]
    for s in range(SWEEPS):
        rcv[s, DEV - 1] = jnp.zeros((1, 128), F32)

    for load in loads[6:]:
        load.wait()
    grid_row = iota((256, 128), 0)
    grid_col = iota((256, 128), 1)
    has_down = (grid_row & 127) < 127
    has_right = grid_col < 127
    conduct = ap[...].reshape(256, 128)
    conduct = conduct * conduct * conduct * (1.0 / 12.0)
    down = jnp.where(has_down, (conduct + pltpu.roll(conduct, 255, 0)) * 0.5, 0.0)
    right_face = jnp.where(has_right, (conduct + pltpu.roll(conduct, 127, 1)) * 0.5, 0.0)
    up = pltpu.roll(down, 1, 0)
    left_face = pltpu.roll(right_face, 1, 1)
    faces = LEAKAGE + (down + up + right_face + left_face)

    wait_bytes(rmsg.at[pl.ds(0, DEV - 1)], m_recv)

    cell = rmsg[:, 0, 0:128].astype(jnp.int32) - 1
    partner = rmsg[:, 0, 256:384]
    parts = [((cell >> 7) + 1).astype(F32), (cell & 127).astype(F32)]
    parts += [x.astype(F32) for x in hilo(rmsg[:, 0, 128:256])]
    hit = [jnp.where(partner[:, s : s + 1] == at_row + 1.0, 1.0, 0.0) for s in range(2)]
    order = jnp.where(at_row < at_col.astype(F32), 1.0, 0.0).astype(BF16)
    first = dot(order, (hit[0] + hit[1]).astype(BF16))
    ahead = [first, first + hit[0]]
    left, right = [], []
    for k in range(2):
        for s in range(2):
            left.append(jnp.where(ahead[s] == float(k), hit[s], 0.0).astype(BF16))
            half = (lane < 64) if k == 0 else (lane >= 64)
            right.append(
                jnp.concatenate(
                    [jnp.where(half, x if k == s else pltpu.roll(x, 64, 1), 0.0).astype(BF16) for x in parts], axis=1
                )
            )
    out = dot(jnp.concatenate(left, axis=0), jnp.concatenate(right, axis=0), 0, 0)
    row1[...] = out[:, 0:128]
    col[...] = out[:, 128:256]
    wgt[...] = out[:, 256:384] + out[:, 384:512]

    row_ids = iota((256, 128), 0).astype(F32) + 1.0
    col_ids = iota((128, 128), 0).astype(F32)

    def lanes(chunk):
        return pl.ds(pl.multiple_of(chunk * (ROWS * 128), ROWS * 128), ROWS * 128)

    def spread(chunk, values):
        tiles = []
        for i in range(ROWS):
            columns = jnp.broadcast_to(col[pl.ds(chunk * ROWS + i, 1), :], (128, 128))
            tiles.append(jnp.where(columns == col_ids, jnp.broadcast_to(values[i], (128, 128)), 0.0).astype(BF16))
        return jnp.concatenate(tiles, axis=1)

    acc[...] = jnp.zeros((256, 128), F32)

    def first_pass(chunk, carry):
        tiles = []
        for i in range(ROWS):
            rows = jnp.broadcast_to(row1[pl.ds(chunk * ROWS + i, 1), :], (256, 128))
            tiles.append(jnp.where(rows == row_ids, 1.0, 0.0).astype(BF16))
        tile = jnp.concatenate(tiles, axis=1)
        hot[:, lanes(chunk)] = tile
        values = [wgt[pl.ds(chunk * ROWS + i, 1), :] for i in range(ROWS)]
        acc[...] += dot(tile, spread(chunk, values), 1, 1)
        return carry

    lax.fori_loop(0, CHUNKS, first_pass, 0)
    inverse = 1.0 / (faces + acc[...])
    inv[...] = inverse
    cdn[...] = down * inverse
    cup[...] = up * inverse
    crt[...] = right_face * inverse
    clf[...] = left_face * inverse
    source = src[...].reshape(256, 128)
    adj[...] = source * inverse

    def sweep(step, carry):
        field = adj[...].T.astype(BF16)
        for chunk in range(CHUNKS):
            picked_rows = dot(field, hot[:, chunk * ROWS * 128 : (chunk + 1) * ROWS * 128])
            for i in range(ROWS):
                r = chunk * ROWS + i
                columns = jnp.broadcast_to(col[r : r + 1, :], (128, 128))
                chosen = jnp.where(columns == col_ids, picked_rows[:, i * 128 : (i + 1) * 128], 0.0)
                snd[step, r] = jnp.sum(chosen, axis=0, keepdims=True)
            for r in range(chunk * ROWS, min((chunk + 1) * ROWS, DEV - 1)):
                pltpu.make_async_remote_copy(
                    src_ref=snd.at[step].at[r],
                    dst_ref=rcv.at[step].at[BACK[r]],
                    send_sem=v_send.at[step],
                    recv_sem=v_recv.at[step].at[chunk],
                    device_id=device_at(ORDER[r], wide, narrow),
                    device_id_type=MESH,
                ).start()
        acc[...] = src[...].reshape(256, 128)
        for chunk in range(CHUNKS):
            count = min(ROWS, DEV - 1 - chunk * ROWS)
            wait_bytes(rcv.at[step].at[pl.ds(chunk * ROWS, count)], v_recv.at[step].at[chunk])
            values = [rcv[step, chunk * ROWS + i] * wgt[chunk * ROWS + i : chunk * ROWS + i + 1, :] for i in range(ROWS)]
            acc[...] += dot(hot[:, chunk * ROWS * 128 : (chunk + 1) * ROWS * 128], spread(chunk, values), 1, 1)
        acc[...] = acc[...] * inv[...]

        def inner(i, carry):
            now = adj[...]
            adj[...] = (
                acc[...]
                + cdn[...] * pltpu.roll(now, 255, 0)
                + cup[...] * pltpu.roll(now, 1, 0)
                + crt[...] * pltpu.roll(now, 127, 1)
                + clf[...] * pltpu.roll(now, 1, 1)
            )
            return carry

        lax.fori_loop(0, INNER, inner, 0)
        return carry

    lax.fori_loop(0, SWEEPS, sweep, 0)
    now = adj[...]
    src[...] = now.reshape(2, 128, 128)
    store = pltpu.make_async_copy(src, adj_h, out_sem.at[0])
    store.start()
    pressure = pr[...].reshape(256, 128)
    aperture = ap[...].reshape(256, 128)
    along_x = jnp.where(has_down, (pressure - pltpu.roll(pressure, 255, 0)) * (now - pltpu.roll(now, 255, 0)), 0.0)
    along_y = jnp.where(has_right, (pressure - pltpu.roll(pressure, 127, 1)) * (now - pltpu.roll(now, 127, 1)), 0.0)
    total = along_x + pltpu.roll(along_x, 1, 0) + along_y + pltpu.roll(along_y, 1, 1)
    grad[...] = (-(aperture * aperture * 0.125) * total).reshape(2, 128, 128)
    store2 = pltpu.make_async_copy(grad, grad_h, out_sem.at[1])
    store2.start()
    wait_bytes(msg.at[pl.ds(0, DEV - 1)], m_send)
    for s in range(SWEEPS):
        wait_bytes(snd.at[s].at[pl.ds(0, DEV - 1)], v_send.at[s])
    store.wait()
    store2.wait()


def body(aperture, pressure, adj_source, trace_weight, end_device, end_local, trace_nodes):
    code_col = jnp.broadcast_to(jnp.asarray(codes())[:, None], (DEV, 128))
    code_row = jnp.broadcast_to(jnp.asarray(codes())[None, :], (8, DEV))
    field = (2, 128, 128)
    any_spec = pl.BlockSpec(memory_space=pl.ANY)
    flat = pltpu.VMEM((256, 128), F32)
    scratch = [
        pltpu.VMEM(field, F32),
        pltpu.VMEM(field, F32),
        pltpu.VMEM(field, F32),
        pltpu.VMEM((64, 64), F32),
        pltpu.VMEM((2, 64), jnp.int32),
        pltpu.VMEM((2, 64), jnp.int32),
        pltpu.VMEM((64, 2, 64), jnp.int32),
        pltpu.VMEM((DEV, 128), jnp.int32),
        pltpu.VMEM((8, DEV), jnp.int32),
        pltpu.SemaphoreType.DMA((9,)),
        pltpu.SemaphoreType.DMA((2,)),
        pltpu.VMEM((DEV, 1, 384), F32),
        pltpu.VMEM((DEV, 1, 384), F32),
        pltpu.VMEM((SWEEPS, DEV, 1, 128), F32),
        pltpu.VMEM((SWEEPS, DEV, 1, 128), F32),
        pltpu.SemaphoreType.DMA,
        pltpu.SemaphoreType.DMA,
        pltpu.SemaphoreType.DMA((SWEEPS,)),
        pltpu.SemaphoreType.DMA((SWEEPS, CHUNKS)),
        pltpu.VMEM((256, DEV * 128), BF16),
        pltpu.VMEM((DEV, 128), F32),
        pltpu.VMEM((DEV, 128), F32),
        pltpu.VMEM((DEV, 128), F32),
        flat, flat, flat, flat, flat, flat, flat,
        pltpu.VMEM(field, F32),
    ]
    return pl.pallas_call(
        kernel,
        out_shape=(jax.ShapeDtypeStruct(field, F32), jax.ShapeDtypeStruct(field, F32)),
        in_specs=[any_spec] * 9,
        out_specs=(any_spec, any_spec),
        scratch_shapes=scratch,
        compiler_params=pltpu.CompilerParams(collective_id=0, has_side_effects=True, vmem_limit_bytes=48 << 20),
    )(aperture, pressure, adj_source, trace_weight, end_device.T, end_local.T, trace_nodes, code_col, code_row)


def solution(mesh):
    line = P(("wide", "narrow"), None)
    cube = P(("wide", "narrow"), None, None)
    return jax.shard_map(
        body,
        mesh=mesh,
        in_specs=(cube, cube, cube, line, line, line, cube),
        out_specs=(cube, cube),
        check_vma=False,
    )
```

time: 252 us -> 68.5 us (0.27)
  other arithmetic: 76.6 us -> 0 us
  waiting for transfers between devices: 69.1 us -> 0 us
  Pallas kernels: 0 us -> 61.3 us
  starting transfers between devices: 43.7 us -> 0 us
  matrix products: 41.5 us -> 0 us
  local copies, waits for them, and re-layouts: 16.2 us -> 6.23 us
  loops' own time: 2.86 us -> 0 us
    all_to_all x8 -> x0, waiting for transfers between devices: 69.1 us -> none  [the longest x3 28.1 us: body(): lax.all_to_all(values, ('wide', 'narrow'), split_axis=0, concat_axis=0, t...]
    pallas_call x0 -> x1, Pallas kernels: none -> 61.3 us  [body(): pl.pallas_call(kernel, out_shape=(jax.ShapeDtypeStruct(field, F32), jax.S...]
    select_n x38 -> x0, other arithmetic: 52 us -> none  [the longest x32 51.9 us: add_block(): jnp.where(col_hot, high_part[:, None], zero_half)]
    all_to_all x8 -> x0, starting transfers between devices: 43.7 us -> none  [the longest x3 13.8 us: body(): lax.all_to_all(packed, ('wide', 'narrow'), split_axis=0, concat_axis=0, t...]
    dot_general x63 -> x0, matrix products: 41.5 us -> none  [the longest x24 25 us: pick_block(): picked = jnp.dot(row_hot, both_parts, preferred_element_type=jnp.float32)]
    mul x82 -> x0, other arithmetic: 8.66 us -> none  [the longest x24 3.16 us: neighbours(): total = total + jnp.pad(face_y * field[:, :, 1:], ((0, 0), (0, 0), (0, 1)))]
    all_to_all x11 -> x0, local copies, waits for them, and re-layouts: 6.76 us -> none  [the longest x3 2.14 us: body(): lax.all_to_all(packed, ('wide', 'narrow'), split_axis=0, concat_axis=0, t...]
    all_to_all x8 -> x0, other arithmetic: 5.8 us -> none  [the longest x3 2.14 us: body(): lax.all_to_all(values, ('wide', 'narrow'), split_axis=0, concat_axis=0, t...]
  transfers between devices with their start and end apart: 8 -> 0, of which waited for: 8 -> 0; matrix products, arithmetic and copies ran while one was open for 2% -> 0% of each run, Pallas kernels for 0% -> 0%
where the time goes in v1:
time: 68.5 us; the launch traced here: 68.2 us
  Pallas kernels  61.3 us (89%)
  local copies, waits for them, and re-layouts  6.23 us (9%)
    pallas_call x1, Pallas kernels, body(): pl.pallas_call(kernel, out_shape=(jax.ShapeDtypeStruct(field, F32), jax.S...  61.3 us
    unnamed x16, local copies, waits for them, and re-layouts  4.79 us

profile of v1, /device:TPU:1, one launch (start us, length us, event | category | flops | bytes accessed | tf_op | source)
XLA Modules:
  0.0 68.2 jit_solution(3975107071005937022)
XLA Ops:
  0.6 0.0 copy-start.3
  0.6 0.7 %broadcast_in_dim.5.kr_h = s32[8,128]{1,0:T(8,128)S(1)} broadcast(s32[128]{0:T(128)} %constant.2.clone), dimensions={1} | broadcast | bytes 4608 | tf_op jit(solution)/shard_map/broadcast_in_dim | solution.py:285
  1.3 0.0 copy-start.5
  1.3 0.0 copy-start.6
  1.3 0.8 %broadcast_in_dim.4.kc_h = s32[128,128]{1,0:T(8,128)S(1)} broadcast(s32[128]{0:T(128)} %constant.2.clone), dimensions={0} | broadcast | bytes 66048 | tf_op jit(solution)/shard_map/broadcast_in_dim | solution.py:284
  2.1 0.0 copy-done.3
  2.1 0.0 copy-done.5
  2.1 0.0 copy-done.6
  2.1 0.0 copy-start
  2.1 0.9 %copy-done = f32[2,128,128]{2,1,0:T(8,128)S(1)} copy-done((f32[2,128,128]{2,1,0:T(8,128)S(1)}, f32[2,128,128]{2,1,0:T(8,128)}, u32[]{:S(2)}) %copy-start) | copy-done | bytes 131096
  3.0 0.0 copy-start.1
  3.0 0.9 %copy-done.1 = f32[2,128,128]{2,1,0:T(8,128)S(1)} copy-done((f32[2,128,128]{2,1,0:T(8,128)S(1)}, f32[2,128,128]{2,1,0:T(8,128)}, u32[]{:S(2)}) %copy-start.1) | copy-done | bytes 131096
  3.9 0.0 copy-start.2
  3.9 0.9 %copy-done.2 = f32[2,128,128]{2,1,0:T(8,128)S(1)} copy-done((f32[2,128,128]{2,1,0:T(8,128)S(1)}, f32[2,128,128]{2,1,0:T(8,128)}, u32[]{:S(2)}) %copy-start.2) | copy-done | bytes 131096
  4.8 0.0 copy-start.4
  4.8 0.8 %copy-done.4 = f32[64,64]{1,0:T(8,128)S(1)} copy-done((f32[64,64]{1,0:T(8,128)S(1)}, f32[64,64]{1,0:T(8,128)}, u32[]{:S(2)}) %copy-start.4) | copy-done | bytes 16408
  5.6 61.3 %shard_map.104 = (f32[2,128,128]{2,1,0:T(8,128)S(1)}, f32[2,128,128]{2,1,0:T(8,128)S(1)}) custom-call(f32[2,128,128]{2,1,0:T(8,128)S(1)} %copy-done, f32[2,128,128]{2,1,0:T(8,128)S(1)} %copy-done.1, f32[2,128,128]{2,1,0:T(8,128)S(1)} %copy-done.2, f32[64,64]{1,0:T(8,128)S(1)} %copy-done.4, s32[2,64]{1,0:T(2,128)S(1)} %bitcast.2, s32[2,64]{1,0:T(2,128)S(1)} %bitcast.3, ...), custom_call_target="tpu_custom_call" | custom-call | tf_op jit(solution)/shard_map/pallas_call | solution.py:316
  66.9 0.7 copy.13
  67.6 0.7 copy.14
Async XLA Ops:
  0.6 1.5 %copy-start.3 = (s32[64,2,64]{2,1,0:T(2,128)S(1)}, s32[64,2,64]{2,1,0:T(2,128)}, u32[]{:S(2)}) copy-start(s32[64,2,64]{2,1,0:T(2,128)} %tn_h.1) | copy-start | bytes 98308
  1.3 0.8 %copy-start.5 = (s32[64,2]{0,1:T(2,128)S(1)}, s32[64,2]{0,1:T(2,128)}, u32[]{:S(2)}) copy-start(s32[64,2]{0,1:T(2,128)} %param.13) | copy-start | bytes 1540
  1.3 0.8 %copy-start.6 = (s32[64,2]{0,1:T(2,128)S(1)}, s32[64,2]{0,1:T(2,128)}, u32[]{:S(2)}) copy-start(s32[64,2]{0,1:T(2,128)} %param.14) | copy-start | bytes 1540
  2.1 0.9 %copy-start = (f32[2,128,128]{2,1,0:T(8,128)S(1)}, f32[2,128,128]{2,1,0:T(8,128)}, u32[]{:S(2)}) copy-start(f32[2,128,128]{2,1,0:T(8,128)} %ap_h.1) | copy-start | bytes 393220
  3.0 0.9 %copy-start.1 = (f32[2,128,128]{2,1,0:T(8,128)S(1)}, f32[2,128,128]{2,1,0:T(8,128)}, u32[]{:S(2)}) copy-start(f32[2,128,128]{2,1,0:T(8,128)} %pr_h.1) | copy-start | bytes 393220
  3.9 0.9 %copy-start.2 = (f32[2,128,128]{2,1,0:T(8,128)S(1)}, f32[2,128,128]{2,1,0:T(8,128)}, u32[]{:S(2)}) copy-start(f32[2,128,128]{2,1,0:T(8,128)} %src_h.1) | copy-start | bytes 393220
  4.8 0.8 %copy-start.4 = (f32[64,64]{1,0:T(8,128)S(1)}, f32[64,64]{1,0:T(8,128)}, u32[]{:S(2)}) copy-start(f32[64,64]{1,0:T(8,128)} %tw_h.1) | copy-start | bytes 49156

commit v2 on v1

--- a/solution.py
+++ b/solution.py
@@ -1,3 +1,4 @@
+import functools
 import itertools
 
 import jax
@@ -27,20 +28,26 @@
     return sum(min(d, 4 - d) for d in offset[:3])
 
 
-def far_first():
-    order = []
-    for offset in sorted(itertools.product(range(4), range(4), range(4), range(2)), key=lambda o: (-hops(o), o)):
-        if offset not in order and negated(offset) != offset:
-            order += [offset, negated(offset)]
-    for offset in itertools.product((0, 2), (0, 2), (0, 2), (0, 1)):
-        order.append(offset)
-    order.sort(key=lambda o: (-hops(o), o == (0, 0, 0, 0)))
-    return order
-
-
-ORDER = far_first()
+def in_groups():
+    every = list(itertools.product(range(4), range(4), range(4), range(2)))
+    every.sort(key=lambda o: (-hops(o), o == HERE))
+    far = [o for o in every if hops(o) > 3]
+    near = [o for o in every if hops(o) < 3]
+    return far + near + [o for o in every if hops(o) == 3]
+
+
+HERE = (0, 0, 0, 0)
+ORDER = in_groups()
+SELF = ORDER.index(HERE)
+OTHERS = sorted((i for i in range(DEV) if i != SELF), key=lambda i: -hops(ORDER[i]))
 BACK = [ORDER.index(negated(o)) for o in ORDER]
-assert all(b // ROWS == i // ROWS for i, b in enumerate(BACK))
+SENT = ((0, 16), (16, 44), (44, 88), (88, 128))
+RECEIVED = ((0, 44), (44, 88), (88, 128))
+HEARD = (1, 0, 2)
+GROUP = [next(g for g, (a, b) in enumerate(RECEIVED) if a <= i < b) for i in range(DEV)]
+assert all(GROUP[b] == GROUP[i] for i, b in enumerate(BACK))
+GATHERED = 2
+SCATTERED = 4
 
 
 def codes():
@@ -81,9 +88,9 @@
 
 
 def kernel(
-    ap_h, pr_h, src_h, tw_h, ed_h, el_h, tn_h, kc_h, kr_h,
+    ap_h, pr_h, src_h, tw_h, ed_h, el_h, tn_h, kr_h,
     grad_h, adj_h,
-    ap, pr, src, tw, ed, el, tn, kc, kr, in_sem, out_sem,
+    ap, pr, src, tw, ed, el, tn, kr, in_sem, out_sem,
     msg, rmsg, snd, rcv, m_send, m_recv, v_send, v_recv,
     hot, row1, col, wgt, adj, cup, cdn, clf, crt, inv, acc, grad,
 ):
@@ -91,19 +98,20 @@
     narrow = lax.axis_index("narrow")
     me = wide * 8 + narrow
     barrier = pltpu.get_barrier_semaphore()
-    for offset in ORDER[:-1]:
-        pl.semaphore_signal(barrier, inc=1, device_id=device_at(offset, wide, narrow), device_id_type=MESH)
-    pairs = [(ed_h, ed), (el_h, el), (tn_h, tn), (tw_h, tw), (kc_h, kc), (kr_h, kr), (ap_h, ap), (src_h, src), (pr_h, pr)]
+    for i in OTHERS:
+        pl.semaphore_signal(barrier, inc=1, device_id=device_at(ORDER[i], wide, narrow), device_id_type=MESH)
+    pairs = [(ed_h, ed), (el_h, el), (tn_h, tn), (tw_h, tw), (kr_h, kr), (ap_h, ap), (src_h, src), (pr_h, pr)]
     loads = [pltpu.make_async_copy(a, b, in_sem.at[i]) for i, (a, b) in enumerate(pairs)]
     for load in loads:
         load.start()
-    for load in loads[:6]:
+    for load in loads[:5]:
         load.wait()
 
-    at_col = moved(kc[...], me)
-    at_row = moved(kr[...], me)[0:1, :].astype(F32)
+    places = moved(kr[...], me).astype(F32)
+    at_row = places[0:1, :]
+    at_col = jnp.broadcast_to(at_row, (DEV, 128)).T
     lane = iota((DEV, 128), 1)
-    member = [jnp.where(at_col[:, :64] == ed[e : e + 1, :], 1.0, 0.0) for e in range(2)]
+    member = [jnp.where(at_col[:, :64] == ed[e : e + 1, :].astype(F32), 1.0, 0.0) for e in range(2)]
     earlier = jnp.where(iota((64, 64), 0) < iota((64, 64), 1), 1.0, 0.0).astype(BF16)
     before = dot((member[0] + member[1]).astype(BF16), earlier)
     place = [[jnp.where(before == float(s), member[e], 0.0) for e in range(2)] for s in range(2)]
@@ -132,20 +140,20 @@
     msg[:, 0, 256:384] = jnp.where(lane == 0, picked(0, other_rows), jnp.where(lane == 1, picked(1, other_rows), 0.0))
 
     pl.semaphore_wait(barrier, DEV - 1)
-    for i, offset in enumerate(ORDER[:-1]):
+    for i in OTHERS:
         pltpu.make_async_remote_copy(
             src_ref=msg.at[i],
             dst_ref=rmsg.at[BACK[i]],
             send_sem=m_send,
             recv_sem=m_recv,
-            device_id=device_at(offset, wide, narrow),
+            device_id=device_at(ORDER[i], wide, narrow),
             device_id_type=MESH,
         ).start()
-    rmsg[DEV - 1] = msg[DEV - 1]
+    rmsg[SELF] = msg[SELF]
     for s in range(SWEEPS):
-        rcv[s, DEV - 1] = jnp.zeros((1, 128), F32)
-
-    for load in loads[6:]:
+        rcv[s, SELF] = jnp.zeros((1, 128), F32)
+
+    for load in loads[5:]:
         load.wait()
     grid_row = iota((256, 128), 0)
     grid_col = iota((256, 128), 1)
@@ -166,7 +174,7 @@
     parts = [((cell >> 7) + 1).astype(F32), (cell & 127).astype(F32)]
     parts += [x.astype(F32) for x in hilo(rmsg[:, 0, 128:256])]
     hit = [jnp.where(partner[:, s : s + 1] == at_row + 1.0, 1.0, 0.0) for s in range(2)]
-    order = jnp.where(at_row < at_col.astype(F32), 1.0, 0.0).astype(BF16)
+    order = jnp.where(at_row < at_col, 1.0, 0.0).astype(BF16)
     first = dot(order, (hit[0] + hit[1]).astype(BF16))
     ahead = [first, first + hit[0]]
     left, right = [], []
@@ -184,34 +192,28 @@
     col[...] = out[:, 128:256]
     wgt[...] = out[:, 256:384] + out[:, 384:512]
 
-    row_ids = iota((256, 128), 0).astype(F32) + 1.0
+    row_ids = (iota((256, 128), 0).astype(F32) + 1.0).astype(BF16)
+    one, nought = jnp.ones((), BF16), jnp.zeros((), BF16)
     col_ids = iota((128, 128), 0).astype(F32)
 
-    def lanes(chunk):
-        return pl.ds(pl.multiple_of(chunk * (ROWS * 128), ROWS * 128), ROWS * 128)
-
-    def spread(chunk, values):
+    def spread(start, values):
+        tiles = []
+        for i, value in enumerate(values):
+            columns = jnp.broadcast_to(col[start + i : start + i + 1, :], (128, 128))
+            tiles.append(jnp.where(columns == col_ids, jnp.broadcast_to(value, (128, 128)), 0.0).astype(BF16))
+        return jnp.concatenate(tiles, axis=1)
+
+    total = faces
+    for chunk in range(CHUNKS):
         tiles = []
         for i in range(ROWS):
-            columns = jnp.broadcast_to(col[pl.ds(chunk * ROWS + i, 1), :], (128, 128))
-            tiles.append(jnp.where(columns == col_ids, jnp.broadcast_to(values[i], (128, 128)), 0.0).astype(BF16))
-        return jnp.concatenate(tiles, axis=1)
-
-    acc[...] = jnp.zeros((256, 128), F32)
-
-    def first_pass(chunk, carry):
-        tiles = []
-        for i in range(ROWS):
-            rows = jnp.broadcast_to(row1[pl.ds(chunk * ROWS + i, 1), :], (256, 128))
-            tiles.append(jnp.where(rows == row_ids, 1.0, 0.0).astype(BF16))
+            rows = jnp.broadcast_to(row1[chunk * ROWS + i : chunk * ROWS + i + 1, :].astype(BF16), (256, 128))
+            tiles.append(jnp.where(rows == row_ids, one, nought))
         tile = jnp.concatenate(tiles, axis=1)
-        hot[:, lanes(chunk)] = tile
-        values = [wgt[pl.ds(chunk * ROWS + i, 1), :] for i in range(ROWS)]
-        acc[...] += dot(tile, spread(chunk, values), 1, 1)
-        return carry
-
-    lax.fori_loop(0, CHUNKS, first_pass, 0)
-    inverse = 1.0 / (faces + acc[...])
+        hot[:, chunk * ROWS * 128 : (chunk + 1) * ROWS * 128] = tile
+        values = [wgt[chunk * ROWS + i : chunk * ROWS + i + 1, :] for i in range(ROWS)]
+        total = total + dot(tile, spread(chunk * ROWS, values), 1, 1)
+    inverse = 1.0 / total
     inv[...] = inverse
     cdn[...] = down * inverse
     cup[...] = up * inverse
@@ -222,29 +224,38 @@
 
     def sweep(step, carry):
         field = adj[...].T.astype(BF16)
-        for chunk in range(CHUNKS):
-            picked_rows = dot(field, hot[:, chunk * ROWS * 128 : (chunk + 1) * ROWS * 128])
-            for i in range(ROWS):
-                r = chunk * ROWS + i
-                columns = jnp.broadcast_to(col[r : r + 1, :], (128, 128))
-                chosen = jnp.where(columns == col_ids, picked_rows[:, i * 128 : (i + 1) * 128], 0.0)
-                snd[step, r] = jnp.sum(chosen, axis=0, keepdims=True)
-            for r in range(chunk * ROWS, min((chunk + 1) * ROWS, DEV - 1)):
-                pltpu.make_async_remote_copy(
-                    src_ref=snd.at[step].at[r],
-                    dst_ref=rcv.at[step].at[BACK[r]],
-                    send_sem=v_send.at[step],
-                    recv_sem=v_recv.at[step].at[chunk],
-                    device_id=device_at(ORDER[r], wide, narrow),
-                    device_id_type=MESH,
-                ).start()
-        acc[...] = src[...].reshape(256, 128)
-        for chunk in range(CHUNKS):
-            count = min(ROWS, DEV - 1 - chunk * ROWS)
-            wait_bytes(rcv.at[step].at[pl.ds(chunk * ROWS, count)], v_recv.at[step].at[chunk])
-            values = [rcv[step, chunk * ROWS + i] * wgt[chunk * ROWS + i : chunk * ROWS + i + 1, :] for i in range(ROWS)]
-            acc[...] += dot(hot[:, chunk * ROWS * 128 : (chunk + 1) * ROWS * 128], spread(chunk, values), 1, 1)
-        acc[...] = acc[...] * inv[...]
+
+        def send(begin, end):
+            for start in range(begin, end, GATHERED):
+                picked_rows = dot(field, hot[:, start * 128 : (start + GATHERED) * 128])
+                for i in range(GATHERED):
+                    r = start + i
+                    columns = jnp.broadcast_to(col[r : r + 1, :], (128, 128))
+                    chosen = jnp.where(columns == col_ids, picked_rows[:, i * 128 : (i + 1) * 128], 0.0)
+                    snd[step, r] = jnp.sum(chosen, axis=0, keepdims=True)
+            for r in range(begin, end):
+                if r != SELF:
+                    pltpu.make_async_remote_copy(
+                        src_ref=snd.at[step].at[r],
+                        dst_ref=rcv.at[step].at[BACK[r]],
+                        send_sem=v_send.at[step],
+                        recv_sem=v_recv.at[step].at[GROUP[r]],
+                        device_id=device_at(ORDER[r], wide, narrow),
+                        device_id_type=MESH,
+                    ).start()
+
+        for begin, end in SENT:
+            pl.when(step < SWEEPS)(functools.partial(send, begin, end))
+
+        total = src[...].reshape(256, 128)
+        for g in HEARD:
+            begin, end = RECEIVED[g]
+            wait_bytes(rcv.at[step].at[pl.ds(begin, end - begin - (begin <= SELF < end))], v_recv.at[step].at[g])
+            for start in range(begin, end, SCATTERED):
+                rows = range(start, start + SCATTERED)
+                values = [rcv[step, r] * wgt[r : r + 1, :] for r in rows]
+                total = total + dot(hot[:, start * 128 : (start + SCATTERED) * 128], spread(start, values), 1, 1)
+        acc[...] = total * inv[...]
 
         def inner(i, carry):
             now = adj[...]
@@ -257,7 +268,7 @@
             )
             return carry
 
-        lax.fori_loop(0, INNER, inner, 0)
+        lax.fori_loop(0, INNER, inner, 0, unroll=True)
         return carry
 
     lax.fori_loop(0, SWEEPS, sweep, 0)
@@ -281,10 +292,9 @@
 
 
 def body(aperture, pressure, adj_source, trace_weight, end_device, end_local, trace_nodes):
-    code_col = jnp.broadcast_to(jnp.asarray(codes())[:, None], (DEV, 128))
-    code_row = jnp.broadcast_to(jnp.asarray(codes())[None, :], (8, DEV))
+    code_row = jnp.asarray(np.tile(codes()[None, :], (8, 1)))
     field = (2, 128, 128)
-    any_spec = pl.BlockSpec(memory_space=pl.ANY)
+    any_spec = pl.BlockSpec(memory_space=pltpu.HBM)
     flat = pltpu.VMEM((256, 128), F32)
     scratch = [
         pltpu.VMEM(field, F32),
@@ -294,9 +304,8 @@
         pltpu.VMEM((2, 64), jnp.int32),
         pltpu.VMEM((2, 64), jnp.int32),
         pltpu.VMEM((64, 2, 64), jnp.int32),
-        pltpu.VMEM((DEV, 128), jnp.int32),
         pltpu.VMEM((8, DEV), jnp.int32),
-        pltpu.SemaphoreType.DMA((9,)),
+        pltpu.SemaphoreType.DMA((8,)),
         pltpu.SemaphoreType.DMA((2,)),
         pltpu.VMEM((DEV, 1, 384), F32),
         pltpu.VMEM((DEV, 1, 384), F32),
@@ -305,7 +314,7 @@
         pltpu.SemaphoreType.DMA,
         pltpu.SemaphoreType.DMA,
         pltpu.SemaphoreType.DMA((SWEEPS,)),
-        pltpu.SemaphoreType.DMA((SWEEPS, CHUNKS)),
+        pltpu.SemaphoreType.DMA((SWEEPS, len(RECEIVED))),
         pltpu.VMEM((256, DEV * 128), BF16),
         pltpu.VMEM((DEV, 128), F32),
         pltpu.VMEM((DEV, 128), F32),
@@ -316,11 +325,11 @@
     return pl.pallas_call(
         kernel,
         out_shape=(jax.ShapeDtypeStruct(field, F32), jax.ShapeDtypeStruct(field, F32)),
-        in_specs=[any_spec] * 9,
+        in_specs=[any_spec] * 8,
         out_specs=(any_spec, any_spec),
         scratch_shapes=scratch,
-        compiler_params=pltpu.CompilerParams(collective_id=0, has_side_effects=True, vmem_limit_bytes=48 << 20),
-    )(aperture, pressure, adj_source, trace_weight, end_device.T, end_local.T, trace_nodes, code_col, code_row)
+        compiler_params=pltpu.CompilerParams(collective_id=0, has_side_effects=True, vmem_limit_bytes=64 << 20),
+    )(aperture, pressure, adj_source, trace_weight, end_device.T, end_local.T, trace_nodes, code_row)
 
 
 def solution(mesh):

time: 68.5 us -> 55.2 us (0.81)
  Pallas kernels: 61.3 us -> 52.1 us
  local copies, waits for them, and re-layouts: 6.23 us -> 2.26 us
    pallas_call x1, Pallas kernels: 61.3 us -> 52.1 us  [body(): pl.pallas_call(kernel, out_shape=(jax.ShapeDtypeStruct(field, F32), jax.S...]
    unnamed x16 -> x4, local copies, waits for them, and re-layouts: 4.79 us -> 2.26 us
    broadcast_in_dim x2 -> x0, local copies, waits for them, and re-layouts: 1.45 us -> none  [the longest x1 0.75 us: body(): code_col = jnp.broadcast_to(jnp.asarray(codes())[:, None], (DEV, 128))]
where the time goes in v2:
time: 55.2 us; the launch traced here: 55 us
  Pallas kernels  52.1 us (94%)
  local copies, waits for them, and re-layouts  2.26 us (4%)
  between operations  0.65 us (1%)
    pallas_call x1, Pallas kernels, body(): pl.pallas_call(kernel, out_shape=(jax.ShapeDtypeStruct(field, F32), jax.S...  52.1 us
    unnamed x4, local copies, waits for them, and re-layouts  2.26 us

profile of v2, /device:TPU:1, one launch (start us, length us, event | category | flops | bytes accessed | tf_op | source)
XLA Modules:
  0.0 55.0 jit_solution(7337316582434641998)
XLA Ops:
  0.6 52.1 %shard_map.95 = (f32[2,128,128]{2,1,0:T(8,128)}, f32[2,128,128]{2,1,0:T(8,128)}) custom-call(f32[2,128,128]{2,1,0:T(8,128)} %ap_h.1, f32[2,128,128]{2,1,0:T(8,128)} %pr_h.1, f32[2,128,128]{2,1,0:T(8,128)} %src_h.1, f32[64,64]{1,0:T(8,128)} %tw_h.1, s32[2,64]{1,0:T(2,128)} %bitcast.2, s32[2,64]{1,0:T(2,128)} %bitcast.3, s32[64,2,64]{2,1,0:T(2,128)} %tn_h.1, ...), custom_call_target="tpu_custom_call" | custom-call | tf_op jit(solution)/shard_map/pallas_call | solution.py:325
  52.8 0.0 copy-start
  52.8 1.6 %copy.12 = f32[2,128,128]{2,1,0:T(8,128)} copy(f32[2,128,128]{2,1,0:T(8,128)} %get-tuple-element.4) | data formatting | bytes 262144
  54.4 0.0 copy-done
  54.4 0.7 %copy.13 = f32[2,128,128]{2,1,0:T(8,128)} copy(f32[2,128,128]{2,1,0:T(8,128)S(1)} %copy-done) | data formatting | bytes 262144
Async XLA Ops:
  52.8 1.6 %copy-start = (f32[2,128,128]{2,1,0:T(8,128)S(1)}, f32[2,128,128]{2,1,0:T(8,128)}, u32[]{:S(2)}) copy-start(f32[2,128,128]{2,1,0:T(8,128)} %get-tuple-element.5) | copy-start | bytes 393220

commit v3 on v2

--- a/solution.py
+++ b/solution.py
@@ -41,7 +41,7 @@
 SELF = ORDER.index(HERE)
 OTHERS = sorted((i for i in range(DEV) if i != SELF), key=lambda i: -hops(ORDER[i]))
 BACK = [ORDER.index(negated(o)) for o in ORDER]
-SENT = ((0, 16), (16, 44), (44, 88), (88, 128))
+SENT = ((44, 88), (0, 44), (88, 128))
 RECEIVED = ((0, 44), (44, 88), (88, 128))
 HEARD = (1, 0, 2)
 GROUP = [next(g for g, (a, b) in enumerate(RECEIVED) if a <= i < b) for i in range(DEV)]
@@ -88,11 +88,11 @@
 
 
 def kernel(
-    ap_h, pr_h, src_h, tw_h, ed_h, el_h, tn_h, kr_h,
-    grad_h, adj_h,
-    ap, pr, src, tw, ed, el, tn, kr, in_sem, out_sem,
+    ap_h, src_h, tw_h, ed_h, el_h, tn_h, kr_h,
+    adj_h,
+    ap, src, tw, ed, el, tn, kr, in_sem, out_sem,
     msg, rmsg, snd, rcv, m_send, m_recv, v_send, v_recv,
-    hot, row1, col, wgt, adj, cup, cdn, clf, crt, inv, acc, grad,
+    hot, row1, col, wgt, adj, cup, cdn, clf, crt, inv, acc,
 ):
     wide = lax.axis_index("wide")
     narrow = lax.axis_index("narrow")
@@ -100,7 +100,7 @@
     barrier = pltpu.get_barrier_semaphore()
     for i in OTHERS:
         pl.semaphore_signal(barrier, inc=1, device_id=device_at(ORDER[i], wide, narrow), device_id_type=MESH)
-    pairs = [(ed_h, ed), (el_h, el), (tn_h, tn), (tw_h, tw), (kr_h, kr), (ap_h, ap), (src_h, src), (pr_h, pr)]
+    pairs = [(ed_h, ed), (el_h, el), (tn_h, tn), (tw_h, tw), (kr_h, kr), (ap_h, ap), (src_h, src)]
     loads = [pltpu.make_async_copy(a, b, in_sem.at[i]) for i, (a, b) in enumerate(pairs)]
     for load in loads:
         load.start()
@@ -245,7 +245,7 @@
                     ).start()
 
         for begin, end in SENT:
-            pl.when(step < SWEEPS)(functools.partial(send, begin, end))
+            pl.when(me < DEV)(functools.partial(send, begin, end))
 
         total = src[...].reshape(256, 128)
         for g in HEARD:
@@ -276,19 +276,23 @@
     src[...] = now.reshape(2, 128, 128)
     store = pltpu.make_async_copy(src, adj_h, out_sem.at[0])
     store.start()
+    wait_bytes(msg.at[pl.ds(0, DEV - 1)], m_send)
+    for s in range(SWEEPS):
+        wait_bytes(snd.at[s].at[pl.ds(0, DEV - 1)], v_send.at[s])
+    store.wait()
+
+
+def finish(ap, pr, adj, grad, out):
+    has_down = (iota((256, 128), 0) & 127) < 127
+    has_right = iota((256, 128), 1) < 127
+    now = adj[...].reshape(256, 128)
+    out[...] = adj[...]
     pressure = pr[...].reshape(256, 128)
     aperture = ap[...].reshape(256, 128)
     along_x = jnp.where(has_down, (pressure - pltpu.roll(pressure, 255, 0)) * (now - pltpu.roll(now, 255, 0)), 0.0)
     along_y = jnp.where(has_right, (pressure - pltpu.roll(pressure, 127, 1)) * (now - pltpu.roll(now, 127, 1)), 0.0)
     total = along_x + pltpu.roll(along_x, 1, 0) + along_y + pltpu.roll(along_y, 1, 1)
     grad[...] = (-(aperture * aperture * 0.125) * total).reshape(2, 128, 128)
-    store2 = pltpu.make_async_copy(grad, grad_h, out_sem.at[1])
-    store2.start()
-    wait_bytes(msg.at[pl.ds(0, DEV - 1)], m_send)
-    for s in range(SWEEPS):
-        wait_bytes(snd.at[s].at[pl.ds(0, DEV - 1)], v_send.at[s])
-    store.wait()
-    store2.wait()
 
 
 def body(aperture, pressure, adj_source, trace_weight, end_device, end_local, trace_nodes):
@@ -299,14 +303,13 @@
     scratch = [
         pltpu.VMEM(field, F32),
         pltpu.VMEM(field, F32),
-        pltpu.VMEM(field, F32),
         pltpu.VMEM((64, 64), F32),
         pltpu.VMEM((2, 64), jnp.int32),
         pltpu.VMEM((2, 64), jnp.int32),
         pltpu.VMEM((64, 2, 64), jnp.int32),
         pltpu.VMEM((8, DEV), jnp.int32),
-        pltpu.SemaphoreType.DMA((8,)),
-        pltpu.SemaphoreType.DMA((2,)),
+        pltpu.SemaphoreType.DMA((7,)),
+        pltpu.SemaphoreType.DMA((1,)),
         pltpu.VMEM((DEV, 1, 384), F32),
         pltpu.VMEM((DEV, 1, 384), F32),
         pltpu.VMEM((SWEEPS, DEV, 1, 128), F32),
@@ -320,16 +323,24 @@
         pltpu.VMEM((DEV, 128), F32),
         pltpu.VMEM((DEV, 128), F32),
         flat, flat, flat, flat, flat, flat, flat,
-        pltpu.VMEM(field, F32),
     ]
-    return pl.pallas_call(
+    shape = jax.ShapeDtypeStruct(field, F32)
+    adjoint = pl.pallas_call(
         kernel,
-        out_shape=(jax.ShapeDtypeStruct(field, F32), jax.ShapeDtypeStruct(field, F32)),
-        in_specs=[any_spec] * 8,
-        out_specs=(any_spec, any_spec),
+        out_shape=shape,
+        in_specs=[any_spec] * 7,
+        out_specs=any_spec,
         scratch_shapes=scratch,
         compiler_params=pltpu.CompilerParams(collective_id=0, has_side_effects=True, vmem_limit_bytes=64 << 20),
-    )(aperture, pressure, adj_source, trace_weight, end_device.T, end_local.T, trace_nodes, code_row)
+    )(aperture, adj_source, trace_weight, end_device.T, end_local.T, trace_nodes, code_row)
+    whole = pl.BlockSpec(memory_space=pltpu.VMEM)
+    return pl.pallas_call(
+        finish,
+        out_shape=(shape, shape),
+        in_specs=[whole] * 3,
+        out_specs=(whole, whole),
+        compiler_params=pltpu.CompilerParams(vmem_limit_bytes=64 << 20),
+    )(aperture, pressure, adjoint)
 
 
 def solution(mesh):

time: 55.2 us -> 53.9 us (0.976)
  local copies, waits for them, and re-layouts: 2.26 us -> 0 us
  Pallas kernels: 52.1 us -> 53.1 us
    unnamed x4 -> x0, local copies, waits for them, and re-layouts: 2.26 us -> none
    pallas_call x1 -> x2, Pallas kernels: 52.1 us -> 53.1 us  [the longest x1 51.2 us: body(): pl.pallas_call(kernel, out_shape=shape, in_specs=[any_spec] * 7, out_spec...]
where the time goes in v3:
time: 53.9 us; the launch traced here: 53.8 us
  Pallas kernels  53.1 us (99%)
  between operations  0.64 us (1%)
    pallas_call x1, Pallas kernels, body(): pl.pallas_call(kernel, out_shape=shape, in_specs=[any_spec] * 7, out_spec...  51.2 us
    pallas_call x1, Pallas kernels, body(): pl.pallas_call(finish, out_shape=(shape, shape), in_specs=[whole] * 3, ou...  1.9 us

profile of v3, /device:TPU:1, one launch (start us, length us, event | category | flops | bytes accessed | tf_op | source)
XLA Modules:
  0.0 53.8 jit_solution(5312857843347178568)
XLA Ops:
  0.6 51.2 %shard_map.95.adj = f32[2,128,128]{2,1,0:T(8,128)} custom-call(f32[2,128,128]{2,1,0:T(8,128)} %ap.1, f32[2,128,128]{2,1,0:T(8,128)} %src_h.1, f32[64,64]{1,0:T(8,128)} %tw_h.1, s32[2,64]{1,0:T(2,128)} %bitcast.2, s32[2,64]{1,0:T(2,128)} %bitcast.3, s32[64,2,64]{2,1,0:T(2,128)} %tn_h.1, s32[8,128]{1,0:T(8,128)} %constant.2.clone.kr_h), custom_call_target="tpu_custom_call" | custom-call | tf_op jit(solution)/shard_map/pallas_call | solution.py:328
  51.9 1.9 %shard_map.96 = (f32[2,128,128]{2,1,0:T(8,128)}, f32[2,128,128]{2,1,0:T(8,128)}) custom-call(f32[2,128,128]{2,1,0:T(8,128)} %ap.1, f32[2,128,128]{2,1,0:T(8,128)} %pr.1, f32[2,128,128]{2,1,0:T(8,128)} %shard_map.95.adj), custom_call_target="tpu_custom_call" | custom-call | tf_op jit(solution)/shard_map/pallas_call | solution.py:337
